TPU v7x, 512 devices: a whole 4x8x8 slice. The times are simulated.
512 devices in a mesh: dp: 64 (over y, x, core), tensor: 8 (over z).
Axes of the slice: x: 4, y: 8, z: 8, core: 2. Of those that a mesh axis runs over, the one named last changes fastest.
Arguments:
- hidden_act: bfloat16 [32768, 1408], P('dp', 'tensor'), may hold values from -6 to 6
- cotangent: bfloat16 [32768, 2048], P('dp', 'tensor'), may hold values from -4 to 4
- down_table: bfloat16 [1408, 64, 2048], P('tensor', 'dp'), may hold values from -0.15625 to 0.15625
- expert_ids: int32 [128, 4], P('dp'), may hold values from 0 to 31, as said below
- merge_weights: float32 [128, 4], P('dp'), may hold values from 0.1 to 1
- owner_slot: int32 [32], replicated, may hold values from 0 to 63, as said below
Outputs:
- layer_out: bfloat16 [32768, 2048], P('dp', 'tensor')
- grad_hidden: bfloat16 [32768, 1408], P('dp', 'tensor')
- expert_grad: float32 [1408, 64, 2048], P('tensor', 'dp')
Inputs may be any that keep to these rules, and one draw needn't show every extreme that they name: `expert_ids`: each segment lists 4 different experts; the 2 segments of one index of dp list exactly 6 different experts together. `owner_slot`: different experts have different slots; slot 63 always holds an expert.
All inputs are finite; a program needn't handle non-finite values.
Results may differ from a plain program's by a relative error of at most 0.013.
Values may be sent and summed in bfloat16 or wider, within the bound.
A program may use at most 128 MiB of HBM per device.

v0:
```python
import jax
import jax.numpy as jnp
from jax import lax
from jax.sharding import PartitionSpec as P

E = 32
K = 4
ROW_PARTS = 4
PAD = 4


def two_pieces(values):
    high = lax.reduce_precision(values, 8, 7)
    low = lax.reduce_precision(values - high, 8, 7)
    return (high, low)


def exchange(blocks):
    return lax.all_to_all(blocks, "dp", split_axis=0, concat_axis=0, tiled=True)


def split_panels(panels, count):
    lead, ff_local, width = panels.shape
    cols = count // ROW_PARTS
    view = panels.reshape(lead, ROW_PARTS, ff_local // ROW_PARTS, cols, width // cols)
    return jnp.transpose(view, (1, 3, 0, 2, 4)).reshape(
        count, lead, ff_local // ROW_PARTS, width // cols
    )


def join_panels(chunks):
    count, lead, rows, lanes = chunks.shape
    cols = count // ROW_PARTS
    view = chunks.reshape(ROW_PARTS, cols, lead, rows, lanes)
    return jnp.transpose(view, (2, 0, 3, 1, 4)).reshape(lead, ROW_PARTS * rows, cols * lanes)


def body(hidden_act, cotangent, down_table, expert_ids, merge_weights, owner_slot):
    count = lax.axis_size("dp")
    seg_count = expert_ids.shape[0]
    ff_local, _, width = down_table.shape
    row_count = hidden_act.shape[0]
    seg_len = row_count // seg_count
    rows = ff_local // ROW_PARTS
    lanes = width * ROW_PARTS // count
    listed = seg_count * K
    full_cot = lax.all_gather(cotangent, "tensor", axis=1, tiled=True)
    high, low = two_pieces(merge_weights)
    meta = jnp.concatenate(
        [expert_ids.astype(jnp.float32).reshape(-1), high.reshape(-1), low.reshape(-1)]
    ).astype(jnp.bfloat16)
    meta = jnp.pad(meta[None, :], ((0, PAD - 1), (0, lanes - 3 * listed)))
    table_chunks = split_panels(jnp.transpose(down_table, (1, 0, 2)), count)[:, 0]
    outgoing = jnp.concatenate(
        [table_chunks, jnp.broadcast_to(meta[None], (count, PAD, lanes))], axis=1
    )
    arrived = exchange(outgoing)
    by_slot = arrived[:, :rows]
    meta_all = arrived[:, rows, : 3 * listed].astype(jnp.float32)
    ids_all = meta_all[:, :listed].astype(jnp.int32).reshape(count * seg_count, K)
    high_all = meta_all[:, listed : 2 * listed].reshape(count * seg_count, K)
    low_all = meta_all[:, 2 * listed :].reshape(count * seg_count, K)
    experts = jnp.arange(E, dtype=jnp.int32)
    slots_all = jnp.sum(
        jnp.where(ids_all[:, :, None] == experts, owner_slot[None, None, :], 0), axis=2
    )
    hits = slots_all[:, :, None] == jnp.arange(count, dtype=jnp.int32)
    coef = jnp.concatenate(
        [
            jnp.sum(jnp.where(hits, high_all[:, :, None], 0.0), axis=1),
            jnp.sum(jnp.where(hits, low_all[:, :, None], 0.0), axis=1),
        ],
        axis=0,
    ).astype(jnp.bfloat16)
    halves = jnp.einsum("ms,srl->mrl", coef, by_slot, preferred_element_type=jnp.float32)
    merged_chunks = (halves[: count * seg_count] + halves[count * seg_count :]).astype(jnp.bfloat16)
    merged = join_panels(exchange(merged_chunks.reshape(count, seg_count, rows, lanes)))
    hidden_seg = hidden_act.reshape(seg_count, seg_len, ff_local)
    cot_seg = full_cot.reshape(seg_count, seg_len, width)
    seg_grads = jnp.einsum(
        "stf,std->sfd", hidden_seg, cot_seg, preferred_element_type=jnp.float32
    ).astype(jnp.bfloat16)
    returned = exchange(split_panels(seg_grads, count)).reshape(count * seg_count, rows, lanes)
    partial_rows = jnp.einsum(
        "stf,sfd->std", hidden_seg, merged, preferred_element_type=jnp.float32
    ).reshape(row_count, width)
    layer_out = lax.psum_scatter(
        partial_rows.astype(jnp.bfloat16), "tensor", scatter_dimension=1, tiled=True
    )
    grad_hidden = (
        jnp.einsum("std,sfd->stf", cot_seg, merged, preferred_element_type=jnp.float32)
        .astype(jnp.bfloat16)
        .reshape(row_count, ff_local)
    )
    by_segment = jnp.stack([coef[: count * seg_count], coef[count * seg_count :]], axis=1)
    slot_halves = jnp.einsum(
        "mhs,mrl->hsrl", by_segment, returned, preferred_element_type=jnp.float32
    )
    slot_grads = (slot_halves[0] + slot_halves[1]).astype(jnp.bfloat16)
    own_grad = join_panels(exchange(slot_grads)[:, None])
    expert_grad = jnp.transpose(own_grad, (1, 0, 2)).astype(jnp.float32)
    return (layer_out, grad_hidden, expert_grad)


def solution(mesh):
    placed = (
        P("dp", "tensor"),
        P("dp", "tensor"),
        P("tensor", "dp", None),
        P("dp", None),
        P("dp", None),
        P(),
    )
    return jax.shard_map(
        body,
        mesh=mesh,
        in_specs=placed,
        out_specs=(P("dp", "tensor"), P("dp", "tensor"), P("tensor", "dp", None)),
        check_vma=False,
    )
```

profile of v0, /device:TPU:1, one launch (start us, length us, event | category | flops | bytes accessed | tf_op | source)
XLA Modules:
  0.0 178.1 jit_solution(396525168196531516)
XLA Ops:
  8.8 1.3 copy.65
  10.4 1.0 pad_maximum_fusion
  11.4 11.8 %all-to-all-start = ((bf16[64,48,128]{2,1,0:T(8,128)(2,1)}), bf16[64,48,128]{2,1,0:T(8,128)(2,1)S(1)}, u32[]{:S(2)}, u32[]{:S(2)}) async-start(bf16[64,48,128]{2,1,0:T(8,128)(2,1)} %pad_maximum_fusion), calls=%async_computation | async-start | bytes 1572864 | tf_op jit(solution)/shard_map/all_to_all | solution.py:19
  23.9 22.0 %all-to-all-done = bf16[64,48,128]{2,1,0:T(8,128)(2,1)S(1)} async-done(((bf16[64,48,128]{2,1,0:T(8,128)(2,1)}), bf16[64,48,128]{2,1,0:T(8,128)(2,1)S(1)}, u32[]{:S(2)}, u32[]{:S(2)}) %all-to-all-start) | async-done | bytes 786464 | tf_op jit(solution)/shard_map/all_to_all | solution.py:19
  46.6 0.9 fusion.4
  48.1 2.1 %copy.51 = bf16[64,2,44,128]{3,1,2,0:T(2,128)(2,1)} copy(bf16[64,2,44,128]{3,1,0,2:T(2,128)(2,1)S(1)} %bitcast.66) | data formatting | bytes 2883584 | tf_op jit(solution)/shard_map/reshape | solution.py:77
  50.2 6.4 %all-to-all-start.1 = ((bf16[64,2,44,128]{3,1,2,0:T(2,128)(2,1)}), bf16[64,2,44,128]{3,1,2,0:T(2,128)(2,1)S(1)}, u32[]{:S(2)}, u32[]{:S(2)}) async-start(bf16[64,2,44,128]{3,1,2,0:T(2,128)(2,1)} %copy.51), calls=%async_computation.1 | async-start | bytes 2883584 | tf_op jit(solution)/shard_map/all_to_all | solution.py:19
  56.6 20.5 %all-gather.2.cloned.1.call-done = bf16[512,2048]{1,0:T(8,128)(2,1)} async-done(((bf16[512,256]{1,0:T(8,128)(2,1)}), bf16[512,2048]{1,0:T(8,128)(2,1)}) %all-gather.2.cloned.1.call-update) | async-done | bytes 2097168 | tf_op jit(solution)/shard_map/all_gather | solution.py:47
  77.1 2.1 %convolution_convert_fusion.1 = bf16[2,176,2048]{2,1,0:T(8,128)(2,1)S(1)} fusion(bf16[2,256,2048]{2,1,0:T(8,128)(2,1)} %bitcast.63, bf16[22,2,8,256]{3,2,1,0:T(8,128)(2,1)S(1)} %bitcast.77), kind=kOutput, calls=%fused_computation.3 | convolution fusion | flops 369819648 | bytes 3719168 | tf_op jit(solution)/shard_map/stf,std->sfd/dot_general | solution.py:80
  80.0 2.6 %copy.57 = bf16[64,2,44,128]{3,1,2,0:T(2,128)(2,1)} copy(bf16[64,2,44,128]{3,0,2,1:T(8,128)(2,1)S(1)} %bitcast.71) | data formatting | bytes 2883584 | tf_op jit(solution)/shard_map/reshape | solution.py:26
  82.6 10.3 %all-to-all-done.1 = bf16[64,2,44,128]{3,1,2,0:T(2,128)(2,1)S(1)} async-done(((bf16[64,2,44,128]{3,1,2,0:T(2,128)(2,1)}), bf16[64,2,44,128]{3,1,2,0:T(2,128)(2,1)S(1)}, u32[]{:S(2)}, u32[]{:S(2)}) %all-to-all-start.1) | async-done | bytes 1441824 | tf_op jit(solution)/shard_map/all_to_all | solution.py:19
  92.9 6.3 %all-to-all-start.2 = ((bf16[64,2,44,128]{3,1,2,0:T(2,128)(2,1)}), bf16[64,2,44,128]{3,1,2,0:T(2,128)(2,1)S(1)}, u32[]{:S(2)}, u32[]{:S(2)}) async-start(bf16[64,2,44,128]{3,1,2,0:T(2,128)(2,1)} %copy.57), calls=%async_computation.3 | async-start | bytes 2883584 | tf_op jit(solution)/shard_map/all_to_all | solution.py:19
  99.4 1.3 copy.78
  100.7 2.5 %reshape.114 = bf16[2,176,2048]{2,1,0:T(8,128)(2,1)S(1)} reshape(bf16[2,4,44,16,128]{4,3,2,1,0:T(8,128)(2,1)} %bitcast.72) | data formatting | bytes 2883584 | tf_op jit(solution)/shard_map/reshape | solution.py:35
  103.2 2.1 %convolution_convert_fusion = bf16[2,2048,256]{1,2,0:T(8,128)(2,1)} fusion(bf16[2,176,2048]{2,1,0:T(8,128)(2,1)S(1)} %reshape.114, bf16[22,2,8,256]{3,2,1,0:T(8,128)(2,1)S(1)} %bitcast.78), kind=kOutput, calls=%fused_computation | convolution fusion | flops 370147328 | bytes 3719168 | tf_op jit(solution)/shard_map/stf,sfd->std/dot_general | solution.py:84
  105.3 30.3 %all-to-all-done.2 = bf16[64,2,44,128]{3,1,2,0:T(2,128)(2,1)S(1)} async-done(((bf16[64,2,44,128]{3,1,2,0:T(2,128)(2,1)}), bf16[64,2,44,128]{3,1,2,0:T(2,128)(2,1)S(1)}, u32[]{:S(2)}, u32[]{:S(2)}) %all-to-all-start.2) | async-done | bytes 1441824 | tf_op jit(solution)/shard_map/all_to_all | solution.py:19
  135.6 1.5 copy.58
  137.9 1.4 copy.59
  139.3 6.5 %all-to-all-start.3 = ((bf16[64,44,128]{2,1,0:T(8,128)(2,1)}), bf16[64,44,128]{2,1,0:T(8,128)(2,1)}, u32[]{:S(2)}, u32[]{:S(2)}) async-start(bf16[64,44,128]{2,1,0:T(8,128)(2,1)} %copy.59), calls=%async_computation.4 | async-start | bytes 1572864 | tf_op jit(solution)/shard_map/all_to_all | solution.py:19
  145.8 0.8 fusion.2
  146.6 0.7 copy.64
  147.3 21.1 %all-to-all-done.3 = bf16[64,44,128]{2,1,0:T(8,128)(2,1)} async-done(((bf16[64,44,128]{2,1,0:T(8,128)(2,1)}), bf16[64,44,128]{2,1,0:T(8,128)(2,1)}, u32[]{:S(2)}, u32[]{:S(2)}) %all-to-all-start.3) | async-done | bytes 720928 | tf_op jit(solution)/shard_map/all_to_all | solution.py:19
  168.5 1.3 convert_bitcast_fusion
  169.7 1.5 copy.60
  (34 shorter events, 5.7 us)
Async XLA Ops:
  11.4 35.1 %copy-start.2 = (s32[32]{0:T(128)S(1)}, s32[32]{0:T(128)}, u32[]{:S(2)}) copy-start(s32[32]{0:T(128)} %param.11) | copy-start | bytes 388
  11.4 34.5 %all-to-all-start = ((bf16[64,48,128]{2,1,0:T(8,128)(2,1)}), bf16[64,48,128]{2,1,0:T(8,128)(2,1)S(1)}, u32[]{:S(2)}, u32[]{:S(2)}) async-start(bf16[64,48,128]{2,1,0:T(8,128)(2,1)} %pad_maximum_fusion), calls=%async_computation | async-start | bytes 1572864 | tf_op jit(solution)/shard_map/all_to_all | solution.py:19
  23.1 54.0 %all-gather.2.cloned.1.call-start = ((), (), s32[]{:S(2)}) async-start(), calls=%async_computation.6 | async-start | bytes 2359296 | tf_op jit(solution)/shard_map/all_gather | solution.py:47
  50.2 26.9 %copy-start.1 = (bf16[512,176]{0,1:T(8,128)(2,1)S(1)}, bf16[512,176]{0,1:T(8,128)(2,1)}, u32[]{:S(2)}) copy-start(bf16[512,176]{0,1:T(8,128)(2,1)} %param.6) | copy-start | bytes 540676
  50.2 42.7 %all-to-all-start.1 = ((bf16[64,2,44,128]{3,1,2,0:T(2,128)(2,1)}), bf16[64,2,44,128]{3,1,2,0:T(2,128)(2,1)S(1)}, u32[]{:S(2)}, u32[]{:S(2)}) async-start(bf16[64,2,44,128]{3,1,2,0:T(2,128)(2,1)} %copy.51), calls=%async_computation.1 | async-start | bytes 2883584 | tf_op jit(solution)/shard_map/all_to_all | solution.py:19
  92.9 42.7 %all-to-all-start.2 = ((bf16[64,2,44,128]{3,1,2,0:T(2,128)(2,1)}), bf16[64,2,44,128]{3,1,2,0:T(2,128)(2,1)S(1)}, u32[]{:S(2)}, u32[]{:S(2)}) async-start(bf16[64,2,44,128]{3,1,2,0:T(2,128)(2,1)} %copy.57), calls=%async_computation.3 | async-start | bytes 2883584 | tf_op jit(solution)/shard_map/all_to_all | solution.py:19
  99.2 72.1 %reduce-scatter.2.cloned.1.call-start = ((), (), s32[]{:S(2)}) async-start(), calls=%async_computation.5 | async-start | bytes 2359296 | tf_op jit(solution)/shard_map/reduce_scatter | solution.py:87
  137.9 7.8 %copy-start = (bf16[512,2048]{1,0:T(8,128)(2,1)S(1)}, bf16[512,2048]{1,0:T(8,128)(2,1)}, u32[]{:S(2)}) copy-start(bf16[512,2048]{1,0:T(8,128)(2,1)} %all-gather.2.cloned.1.call-done) | copy-start | bytes 6291460
  139.3 29.2 %all-to-all-start.3 = ((bf16[64,44,128]{2,1,0:T(8,128)(2,1)}), bf16[64,44,128]{2,1,0:T(8,128)(2,1)}, u32[]{:S(2)}, u32[]{:S(2)}) async-start(bf16[64,44,128]{2,1,0:T(8,128)(2,1)} %copy.59), calls=%async_computation.4 | async-start | bytes 1572864 | tf_op jit(solution)/shard_map/all_to_all | solution.py:19
Sparse Core Ops, SparseCore 0:
  26.0 51.0 all-gather.1
  105.4 45.6 reduce-scatter.1
where the time goes:
time: 179 us; the launch traced here: 178 us
  waiting for transfers between devices  105 us (59%)
  starting transfers between devices  31.1 us (17%)
  local copies, waits for them, and re-layouts  16.5 us (9%)
  between operations  14.2 us (8%)
  matrix products  6.5 us (4%)
  other arithmetic  4.78 us (3%)
    all_to_all x4, waiting for transfers between devices, exchange(): return lax.all_to_all(blocks, 'dp', split_axis=0, concat_axis=0, tiled=True)  83.7 us
    all_to_all x4, starting transfers between devices, exchange(): return lax.all_to_all(blocks, 'dp', split_axis=0, concat_axis=0, tiled=True)  30.9 us
    all_gather x1, waiting for transfers between devices, body(): full_cot = lax.all_gather(cotangent, 'tensor', axis=1, tiled=True)  20.5 us
  transfers between devices with their start and end apart: 6, of which 5 were waited for; matrix products, arithmetic and copies ran while one was open for 13% of the time, Pallas kernels for 0%

commit v1 on v0

--- a/solution.py
+++ b/solution.py
@@ -44,7 +44,14 @@
     rows = ff_local // ROW_PARTS
     lanes = width * ROW_PARTS // count
     listed = seg_count * K
-    full_cot = lax.all_gather(cotangent, "tensor", axis=1, tiled=True)
+    ring = [cotangent]
+    for hop in range(7):
+        ring.append(lax.ppermute(ring[-1], "tensor", [(dev, (dev + 1) % 8) for dev in range(8)]))
+    full_cot = jnp.roll(
+        jnp.concatenate(ring[::-1], axis=1),
+        (lax.axis_index("tensor") + 1) * ring[0].shape[1],
+        axis=1,
+    )
     high, low = two_pieces(merge_weights)
     meta = jnp.concatenate(
         [expert_ids.astype(jnp.float32).reshape(-1), high.reshape(-1), low.reshape(-1)]

time: 179 us -> 222 us (1.24)
  starting transfers between devices: 31.1 us -> 55.5 us
  waiting for transfers between devices: 105 us -> 121 us
  local copies, waits for them, and re-layouts: 16.5 us -> 19 us
    ppermute x0 -> x7, waiting for transfers between devices: none -> 50 us  [body(): lax.ppermute(ring[-1], 'tensor', [(dev, (dev + 1) % 8) for dev in range(8)])]
    all_gather x1 -> x0, waiting for transfers between devices: 20.5 us -> none  [body(): full_cot = lax.all_gather(cotangent, 'tensor', axis=1, tiled=True)]
    ppermute x0 -> x7, starting transfers between devices: none -> 15.5 us  [body(): lax.ppermute(ring[-1], 'tensor', [(dev, (dev + 1) % 8) for dev in range(8)])]
    all_to_all x4, waiting for transfers between devices: 83.7 us -> 70.5 us  [exchange(): return lax.all_to_all(blocks, 'dp', split_axis=0, concat_axis=0, tiled=True)]
    all_to_all x4, starting transfers between devices: 30.9 us -> 39.8 us  [exchange(): return lax.all_to_all(blocks, 'dp', split_axis=0, concat_axis=0, tiled=True)]
  transfers between devices with their start and end apart: 6 -> 12, of which waited for: 5 -> 9; matrix products, arithmetic and copies ran while one was open for 13% -> 12% of each run, Pallas kernels for 0% -> 0%
where the time goes in v1:
time: 222 us; the launch traced here: 221 us
  waiting for transfers between devices  121 us (55%)
  starting transfers between devices  55.5 us (25%)
  local copies, waits for them, and re-layouts  19 us (9%)
  between operations  14.5 us (7%)
  matrix products  6.57 us (3%)
  other arithmetic  4.82 us (2%)
    all_to_all x4, waiting for transfers between devices, exchange(): return lax.all_to_all(blocks, 'dp', split_axis=0, concat_axis=0, tiled=True)  70.5 us
    ppermute x7, waiting for transfers between devices, body(): lax.ppermute(ring[-1], 'tensor', [(dev, (dev + 1) % 8) for dev in range(8)])  50 us
    all_to_all x4, starting transfers between devices, exchange(): return lax.all_to_all(blocks, 'dp', split_axis=0, concat_axis=0, tiled=True)  39.8 us
    ppermute x7, starting transfers between devices, body(): lax.ppermute(ring[-1], 'tensor', [(dev, (dev + 1) % 8) for dev in range(8)])  15.5 us
  transfers between devices with their start and end apart: 12, of which 9 were waited for; matrix products, arithmetic and copies ran while one was open for 12% of the time, Pallas kernels for 0%

profile of v1, /device:TPU:1, one launch (start us, length us, event | category | flops | bytes accessed | tf_op | source)
XLA Modules:
  0.0 220.9 jit_solution(5024835127686759877)
XLA Ops:
  11.4 11.6 %all-to-all-start = ((bf16[64,48,128]{2,1,0:T(8,128)(2,1)}), bf16[64,48,128]{2,1,0:T(8,128)(2,1)S(1)}, u32[]{:S(2)}, u32[]{:S(2)}) async-start(bf16[64,48,128]{2,1,0:T(8,128)(2,1)} %pad_maximum_fusion), calls=%async_computation | async-start | bytes 1572864 | tf_op jit(solution)/shard_map/all_to_all | solution.py:19
  23.1 4.0 %collective-permute-start = (bf16[512,256]{1,0:T(8,128)(2,1)S(1)}, bf16[512,256]{1,0:T(8,128)(2,1)S(1)}, u32[]{:S(2)}, u32[]{:S(2)}) collective-permute-start(bf16[512,256]{1,0:T(8,128)(2,1)S(1)} %copy-done), channel_id=1, source_target_pairs={{0,1},{1,2},{2,3},{3,4},{4,5},{5,6},{6,7},{7,0},{8,9},{9,10},{10,1... | collective-permute-start | bytes 786440 | tf_op jit(solution)/shard_map/ppermute | solution.py:49
  27.1 12.9 %collective-permute-done = bf16[512,256]{1,0:T(8,128)(2,1)S(1)} collective-permute-done((bf16[512,256]{1,0:T(8,128)(2,1)S(1)}, bf16[512,256]{1,0:T(8,128)(2,1)S(1)}, u32[]{:S(2)}, u32[]{:S(2)}) %collective-permute-start) | collective-permute-done | bytes 262176 | tf_op jit(solution)/shard_map/ppermute | solution.py:49
  40.0 1.9 collective-permute-start.1
  41.9 8.0 %collective-permute-done.1 = bf16[512,256]{1,0:T(8,128)(2,1)S(1)} collective-permute-done((bf16[512,256]{1,0:T(8,128)(2,1)S(1)}, bf16[512,256]{1,0:T(8,128)(2,1)S(1)}, u32[]{:S(2)}, u32[]{:S(2)}) %collective-permute-start.1) | collective-permute-done | bytes 262176 | tf_op jit(solution)/shard_map/ppermute | solution.py:49
  49.9 1.9 collective-permute-start.2
  51.8 7.1 %collective-permute-done.2 = bf16[512,256]{1,0:T(8,128)(2,1)S(1)} collective-permute-done((bf16[512,256]{1,0:T(8,128)(2,1)S(1)}, bf16[512,256]{1,0:T(8,128)(2,1)S(1)}, u32[]{:S(2)}, u32[]{:S(2)}) %collective-permute-start.2) | collective-permute-done | bytes 262176 | tf_op jit(solution)/shard_map/ppermute | solution.py:49
  58.9 1.9 collective-permute-start.3
  60.8 6.4 %collective-permute-done.3 = bf16[512,256]{1,0:T(8,128)(2,1)S(1)} collective-permute-done((bf16[512,256]{1,0:T(8,128)(2,1)S(1)}, bf16[512,256]{1,0:T(8,128)(2,1)S(1)}, u32[]{:S(2)}, u32[]{:S(2)}) %collective-permute-start.3) | collective-permute-done | bytes 262176 | tf_op jit(solution)/shard_map/ppermute | solution.py:49
  67.2 1.9 collective-permute-start.4
  69.2 6.4 %collective-permute-done.4 = bf16[512,256]{1,0:T(8,128)(2,1)S(1)} collective-permute-done((bf16[512,256]{1,0:T(8,128)(2,1)S(1)}, bf16[512,256]{1,0:T(8,128)(2,1)S(1)}, u32[]{:S(2)}, u32[]{:S(2)}) %collective-permute-start.4) | collective-permute-done | bytes 262176 | tf_op jit(solution)/shard_map/ppermute | solution.py:49
  79.7 2.1 copy.51
  81.8 15.3 %all-to-all-start.1 = ((bf16[64,2,44,128]{3,1,2,0:T(2,128)(2,1)}), bf16[64,2,44,128]{3,1,2,0:T(2,128)(2,1)S(1)}, u32[]{:S(2)}, u32[]{:S(2)}) async-start(bf16[64,2,44,128]{3,1,2,0:T(2,128)(2,1)} %copy.51), calls=%async_computation.1 | async-start | bytes 2883584 | tf_op jit(solution)/shard_map/all_to_all | solution.py:19
  97.1 1.9 collective-permute-start.6
  99.1 9.2 %collective-permute-done.6 = bf16[512,256]{1,0:T(8,128)(2,1)S(1)} collective-permute-done((bf16[512,256]{1,0:T(8,128)(2,1)S(1)}, bf16[512,256]{1,0:T(8,128)(2,1)S(1)}, u32[]{:S(2)}, u32[]{:S(2)}) %collective-permute-start.6) | collective-permute-done | bytes 262176 | tf_op jit(solution)/shard_map/ppermute | solution.py:49
  110.8 2.6 %copy.57 = bf16[64,2,44,128]{3,1,2,0:T(2,128)(2,1)} copy(bf16[64,2,44,128]{3,0,2,1:T(8,128)(2,1)S(1)} %bitcast.71) | data formatting | bytes 2883584 | tf_op jit(solution)/shard_map/reshape | solution.py:26
  113.4 20.1 %all-to-all-done.1 = bf16[64,2,44,128]{3,1,2,0:T(2,128)(2,1)S(1)} async-done(((bf16[64,2,44,128]{3,1,2,0:T(2,128)(2,1)}), bf16[64,2,44,128]{3,1,2,0:T(2,128)(2,1)S(1)}, u32[]{:S(2)}, u32[]{:S(2)}) %all-to-all-start.1) | async-done | bytes 1441824 | tf_op jit(solution)/shard_map/all_to_all | solution.py:19
  133.5 6.5 %all-to-all-start.2 = ((bf16[64,2,44,128]{3,1,2,0:T(2,128)(2,1)}), bf16[64,2,44,128]{3,1,2,0:T(2,128)(2,1)}, u32[]{:S(2)}, u32[]{:S(2)}) async-start(bf16[64,2,44,128]{3,1,2,0:T(2,128)(2,1)} %copy.57), calls=%async_computation.3 | async-start | bytes 2883584 | tf_op jit(solution)/shard_map/all_to_all | solution.py:19
  141.4 2.5 %reshape.114 = bf16[2,176,2048]{2,1,0:T(8,128)(2,1)S(1)} reshape(bf16[2,4,44,16,128]{4,3,2,1,0:T(8,128)(2,1)} %bitcast.72) | data formatting | bytes 2883584 | tf_op jit(solution)/shard_map/reshape | solution.py:35
  143.9 3.0 %convolution_convert_fusion = bf16[2,2048,256]{1,2,0:T(8,128)(2,1)} fusion(bf16[2,176,2048]{2,1,0:T(8,128)(2,1)S(1)} %reshape.114, bf16[22,2,8,256]{3,2,1,0:T(8,128)(2,1)} %bitcast.77), kind=kOutput, calls=%fused_computation | convolution fusion | flops 370147328 | bytes 3719168 | tf_op jit(solution)/shard_map/stf,sfd->std/dot_general | solution.py:91
  146.9 29.3 %all-to-all-done.2 = bf16[64,2,44,128]{3,1,2,0:T(2,128)(2,1)} async-done(((bf16[64,2,44,128]{3,1,2,0:T(2,128)(2,1)}), bf16[64,2,44,128]{3,1,2,0:T(2,128)(2,1)}, u32[]{:S(2)}, u32[]{:S(2)}) %all-to-all-start.2) | async-done | bytes 1441824 | tf_op jit(solution)/shard_map/all_to_all | solution.py:19
  176.2 2.9 %copy.58 = bf16[64,2,44,128]{3,1,0,2:T(2,128)(2,1)S(1)} copy(bf16[64,2,44,128]{3,1,2,0:T(2,128)(2,1)} %all-to-all-done.2) | data formatting | bytes 2883584 | tf_op jit(solution)/shard_map/all_to_all | solution.py:19
  182.0 6.5 %all-to-all-start.3 = ((bf16[64,44,128]{2,1,0:T(8,128)(2,1)}), bf16[64,44,128]{2,1,0:T(8,128)(2,1)}, u32[]{:S(2)}, u32[]{:S(2)}) async-start(bf16[64,44,128]{2,1,0:T(8,128)(2,1)} %copy.59), calls=%async_computation.4 | async-start | bytes 1572864 | tf_op jit(solution)/shard_map/all_to_all | solution.py:19
  190.0 21.2 %all-to-all-done.3 = bf16[64,44,128]{2,1,0:T(8,128)(2,1)} async-done(((bf16[64,44,128]{2,1,0:T(8,128)(2,1)}), bf16[64,44,128]{2,1,0:T(8,128)(2,1)}, u32[]{:S(2)}, u32[]{:S(2)}) %all-to-all-start.3) | async-done | bytes 720928 | tf_op jit(solution)/shard_map/all_to_all | solution.py:19
  (64 shorter events, 19.5 us)
Async XLA Ops:
  7.2 15.9 %copy-start = (bf16[512,256]{1,0:T(8,128)(2,1)S(1)}, bf16[512,256]{1,0:T(8,128)(2,1)}, u32[]{:S(2)}) copy-start(bf16[512,256]{1,0:T(8,128)(2,1)} %param.7) | copy-start | bytes 786436
  7.2 70.9 %copy-start.3 = (s32[32]{0:T(128)S(1)}, s32[32]{0:T(128)}, u32[]{:S(2)}) copy-start(s32[32]{0:T(128)} %param.11) | copy-start | bytes 388
  11.4 66.1 %all-to-all-start = ((bf16[64,48,128]{2,1,0:T(8,128)(2,1)}), bf16[64,48,128]{2,1,0:T(8,128)(2,1)S(1)}, u32[]{:S(2)}, u32[]{:S(2)}) async-start(bf16[64,48,128]{2,1,0:T(8,128)(2,1)} %pad_maximum_fusion), calls=%async_computation | async-start | bytes 1572864 | tf_op jit(solution)/shard_map/all_to_all | solution.py:19
  23.1 16.9 %collective-permute-start = (bf16[512,256]{1,0:T(8,128)(2,1)S(1)}, bf16[512,256]{1,0:T(8,128)(2,1)S(1)}, u32[]{:S(2)}, u32[]{:S(2)}) collective-permute-start(bf16[512,256]{1,0:T(8,128)(2,1)S(1)} %copy-done), channel_id=1, source_target_pairs={{0,1},{1,2},{2,3},{3,4},{4,5},{5,6},{6,7},{7,0},{8,9},{9,10},{10,1... | collective-permute-start | bytes 786440 | tf_op jit(solution)/shard_map/ppermute | solution.py:49
  40.0 9.9 %collective-permute-start.1 = (bf16[512,256]{1,0:T(8,128)(2,1)S(1)}, bf16[512,256]{1,0:T(8,128)(2,1)S(1)}, u32[]{:S(2)}, u32[]{:S(2)}) collective-permute-start(bf16[512,256]{1,0:T(8,128)(2,1)S(1)} %collective-permute-done), channel_id=1, source_target_pairs={{0,1},{1,2},{2,3},{3,4},{4,5},{5,6},{6,7},{7,0},{8,9},{9,10},{10,1... | collective-permute-start | bytes 786440 | tf_op jit(solution)/shard_map/ppermute | solution.py:49
  49.9 9.0 %collective-permute-start.2 = (bf16[512,256]{1,0:T(8,128)(2,1)S(1)}, bf16[512,256]{1,0:T(8,128)(2,1)S(1)}, u32[]{:S(2)}, u32[]{:S(2)}) collective-permute-start(bf16[512,256]{1,0:T(8,128)(2,1)S(1)} %collective-permute-done.1), channel_id=1, source_target_pairs={{0,1},{1,2},{2,3},{3,4},{4,5},{5,6},{6,7},{7,0},{8,9},{9,10},{10,1... | collective-permute-start | bytes 786440 | tf_op jit(solution)/shard_map/ppermute | solution.py:49
  58.9 8.3 %collective-permute-start.3 = (bf16[512,256]{1,0:T(8,128)(2,1)S(1)}, bf16[512,256]{1,0:T(8,128)(2,1)S(1)}, u32[]{:S(2)}, u32[]{:S(2)}) collective-permute-start(bf16[512,256]{1,0:T(8,128)(2,1)S(1)} %collective-permute-done.2), channel_id=1, source_target_pairs={{0,1},{1,2},{2,3},{3,4},{4,5},{5,6},{6,7},{7,0},{8,9},{9,10},{10,1... | collective-permute-start | bytes 786440 | tf_op jit(solution)/shard_map/ppermute | solution.py:49
  67.2 8.3 %collective-permute-start.4 = (bf16[512,256]{1,0:T(8,128)(2,1)S(1)}, bf16[512,256]{1,0:T(8,128)(2,1)S(1)}, u32[]{:S(2)}, u32[]{:S(2)}) collective-permute-start(bf16[512,256]{1,0:T(8,128)(2,1)S(1)} %collective-permute-done.3), channel_id=1, source_target_pairs={{0,1},{1,2},{2,3},{3,4},{4,5},{5,6},{6,7},{7,0},{8,9},{9,10},{10,1... | collective-permute-start | bytes 786440 | tf_op jit(solution)/shard_map/ppermute | solution.py:49
  75.6 21.5 %collective-permute-start.5 = (bf16[512,256]{1,0:T(8,128)(2,1)S(1)}, bf16[512,256]{1,0:T(8,128)(2,1)S(1)}, u32[]{:S(2)}, u32[]{:S(2)}) collective-permute-start(bf16[512,256]{1,0:T(8,128)(2,1)S(1)} %collective-permute-done.4), channel_id=1, source_target_pairs={{0,1},{1,2},{2,3},{3,4},{4,5},{5,6},{6,7},{7,0},{8,9},{9,10},{10,1... | collective-permute-start | bytes 786440 | tf_op jit(solution)/shard_map/ppermute | solution.py:49
  78.2 1.5 copy-start.2
  81.8 51.6 %all-to-all-start.1 = ((bf16[64,2,44,128]{3,1,2,0:T(2,128)(2,1)}), bf16[64,2,44,128]{3,1,2,0:T(2,128)(2,1)S(1)}, u32[]{:S(2)}, u32[]{:S(2)}) async-start(bf16[64,2,44,128]{3,1,2,0:T(2,128)(2,1)} %copy.51), calls=%async_computation.1 | async-start | bytes 2883584 | tf_op jit(solution)/shard_map/all_to_all | solution.py:19
  97.1 11.1 %collective-permute-start.6 = (bf16[512,256]{1,0:T(8,128)(2,1)S(1)}, bf16[512,256]{1,0:T(8,128)(2,1)S(1)}, u32[]{:S(2)}, u32[]{:S(2)}) collective-permute-start(bf16[512,256]{1,0:T(8,128)(2,1)S(1)} %collective-permute-done.5), channel_id=1, source_target_pairs={{0,1},{1,2},{2,3},{3,4},{4,5},{5,6},{6,7},{7,0},{8,9},{9,10},{10,1... | collective-permute-start | bytes 786440 | tf_op jit(solution)/shard_map/ppermute | solution.py:49
  108.5 0.9 copy-start.1
  133.5 42.8 %all-to-all-start.2 = ((bf16[64,2,44,128]{3,1,2,0:T(2,128)(2,1)}), bf16[64,2,44,128]{3,1,2,0:T(2,128)(2,1)}, u32[]{:S(2)}, u32[]{:S(2)}) async-start(bf16[64,2,44,128]{3,1,2,0:T(2,128)(2,1)} %copy.57), calls=%async_computation.3 | async-start | bytes 2883584 | tf_op jit(solution)/shard_map/all_to_all | solution.py:19
  139.9 74.1 %reduce-scatter.2.cloned.1.call-start = ((), (), s32[]{:S(2)}) async-start(), calls=%async_computation.5 | async-start | bytes 2359296 | tf_op jit(solution)/shard_map/reduce_scatter | solution.py:94
  182.0 29.2 %all-to-all-start.3 = ((bf16[64,44,128]{2,1,0:T(8,128)(2,1)}), bf16[64,44,128]{2,1,0:T(8,128)(2,1)}, u32[]{:S(2)}, u32[]{:S(2)}) async-start(bf16[64,44,128]{2,1,0:T(8,128)(2,1)} %copy.59), calls=%async_computation.4 | async-start | bytes 1572864 | tf_op jit(solution)/shard_map/all_to_all | solution.py:19
Sparse Core Ops, SparseCore 0:
  147.1 39.7 reduce-scatter.1
